TPU v7x, 32 devices: a whole 2x2x4 slice. The times are simulated.
32 devices in a mesh: energy: 8 (over y, x, core), kpt: 4 (over z).
Axes of the slice: x: 2, y: 2, z: 4, core: 2. Of those that a mesh axis runs over, the one named last changes fastest.
Arguments:
- density: bfloat16 [32, 4, 64, 3072], P('energy', 'kpt'), may hold values from -6 to 6
- quad_weights: float32 [32, 4], P('energy', 'kpt'), may hold values from 0.044194173 to 0.17677669
- orbital_cells: int32 [64, 3072], replicated, may hold values from 0 to 131071
- fixed_charge: float32 [512, 64, 256], P('energy', 'kpt'), may hold values from -16 to 16
- gate_mask: int32 [512, 64, 256], P('energy', 'kpt'), may hold values 0 or 1
- gate_voltage: float32 [512], P('energy'), may hold values from -1 to 1
Outputs:
- potential: float32 [512, 64, 256], P('energy', 'kpt')
- band_shift: float32 [32, 4, 64], P('energy', 'kpt')
Inputs may be any that keep to these rules, and one draw needn't show every extreme that they name: `orbital_cells`: each entry is s * 64 * 256 + y * 256 + z, a cell of one of the layer's 8 planes.
All inputs are finite; a program needn't handle non-finite values. No bound on the sum of `gate_mask` on one device may be relied on, other than what follows from the above.
Results may differ from a plain program's by a relative error of at most 0.0003.
Values sent between devices are 32-bit elements; how exact they have to be, the bound alone decides.
A program may use at most 64 MiB of HBM per device.

v0:
```python
import jax
import jax.numpy as jnp
from jax import lax
from jax.sharding import PartitionSpec as P

LAYER_DEV = 8
SUB = 8
ITERS = 2
PENALTY = 4.0


def with_halo(block, sides, width):
    for axis, dim in sides:
        count = lax.axis_size(axis)
        forward = [(i, i + 1) for i in range(count - 1)]
        backward = [(target, source) for source, target in forward]
        low = lax.ppermute(
            lax.slice_in_dim(block, block.shape[dim] - width, None, axis=dim), axis, forward
        )
        high = lax.ppermute(lax.slice_in_dim(block, 0, width, axis=dim), axis, backward)
        block = jnp.concatenate([low, block, high], axis=dim)
    return block


def operate(values_field, diagonal):
    padded = with_halo(values_field, (("energy", 0), ("kpt", 1)), 1)
    padded = jnp.pad(padded, ((0, 0), (0, 0), (1, 1)))
    beside = padded[2:, 1:-1, 1:-1] + padded[:-2, 1:-1, 1:-1]
    beside = beside + padded[1:-1, 2:, 1:-1] + padded[1:-1, :-2, 1:-1]
    beside = beside + padded[1:-1, 1:-1, 2:] + padded[1:-1, 1:-1, :-2]
    return diagonal * values_field - beside


def paired_sums(residual, image):
    return lax.psum((jnp.sum(residual * residual), jnp.sum(residual * image)), ("energy", "kpt"))


def window_index(map_rows, kpt_index, planes, cross_y, width_y, depth_z):
    section = cross_y * depth_z
    within = map_rows % section
    column = within // depth_z - kpt_index * width_y
    inside = (column >= 0) & (column < width_y)
    layer_rows = lax.broadcasted_iota(jnp.int32, map_rows.shape, 0)
    flat_cell = (
        (layer_rows * planes + map_rows // section) * width_y + jnp.clip(column, 0, width_y - 1)
    ) * depth_z + within % depth_z
    return (flat_cell, inside)


def per_device(density, quad_weights, orbital_cells, fixed_charge, gate_mask, gate_voltage):
    planes_dev, width_y, depth_z = fixed_charge.shape
    kpt_index = lax.axis_index("kpt")
    cross_y = width_y * lax.axis_size("kpt")
    occupancy = jnp.einsum(
        "ek,eklo->lo", quad_weights, density.astype(jnp.float32), precision=lax.Precision.HIGHEST
    )
    partial_rows = lax.psum_scatter(occupancy, "energy", scatter_dimension=0, tiled=True)
    slab_occupancy = lax.psum(partial_rows, "kpt")
    slab_cells = lax.dynamic_slice_in_dim(
        orbital_cells, lax.axis_index("energy") * LAYER_DEV, LAYER_DEV, 0
    )
    flat_cell, inside = window_index(slab_cells, kpt_index, SUB, cross_y, width_y, depth_z)
    deposit = jax.ops.segment_sum(
        jnp.where(inside, slab_occupancy, 0.0).reshape(-1),
        flat_cell.reshape(-1),
        num_segments=planes_dev * width_y * depth_z,
    )
    charge = deposit.reshape(planes_dev, width_y, depth_z)
    gated = gate_mask.astype(jnp.float32)
    diagonal = 6.0 + PENALTY * gated
    right_side = fixed_charge - charge + PENALTY * gated * gate_voltage[:, None, None]
    potential = jnp.zeros_like(right_side)
    residual = right_side
    image = operate(residual, diagonal)
    norm_now, product = paired_sums(residual, image)
    alpha = norm_now / product
    direction = residual
    along = image
    for sweep_index in range(ITERS):
        potential = potential + alpha * direction
        residual = residual - alpha * along
        if sweep_index + 1 < ITERS:
            image = operate(residual, diagonal)
            norm_next, product = paired_sums(residual, image)
            ratio = norm_next / norm_now
            alpha = norm_next / (product - ratio * norm_next / alpha)
            direction = residual + ratio * direction
            along = image + ratio * along
            norm_now = norm_next
    local_values = jnp.where(inside, jnp.take(potential.reshape(-1), flat_cell), 0.0)
    orbital_potential = lax.psum(local_values, "kpt")
    factor = density.shape[3] ** (-0.5)
    block = density.astype(jnp.float32)
    band_shift = (
        jnp.einsum(
            "eklo,lo->ekl",
            block,
            lax.all_gather(orbital_potential, "energy", axis=0, tiled=True),
            precision=lax.Precision.HIGHEST,
        )
        * factor
    )
    return (potential, band_shift)


def solution(mesh):
    in_specs = (
        P("energy", "kpt", None, None),
        P("energy", "kpt"),
        P(),
        P("energy", "kpt", None),
        P("energy", "kpt", None),
        P("energy"),
    )
    out_specs = (P("energy", "kpt", None), P("energy", "kpt", None))
    return jax.shard_map(
        per_device, mesh=mesh, in_specs=in_specs, out_specs=out_specs, check_vma=False
    )
```

profile of v0, /device:TPU:0, one launch (start us, length us, event | category | flops | bytes accessed | tf_op | source)
XLA Modules:
  0.0 549.4 jit_solution(11437265235670384205)
XLA Ops:
  7.2 1.4 copy-done
  8.6 3.8 fusion.3
  13.5 1.1 fusion.26
  14.6 36.6 %reduce-scatter.2.cloned.1.call-done = f32[8,3072]{1,0:T(8,128)} async-done(((f32[64,3072]{1,0:T(8,128)}), f32[8,3072]{1,0:T(8,128)}) %reduce-scatter.2.cloned.1.call-update) | async-done | bytes 98320 | tf_op jit(solution)/shard_map/reduce_scatter | solution.py:57
  51.3 36.7 %all-reduce.7.cloned.1.call-done = f32[8,3072]{1,0:T(8,128)} async-done(((f32[8,3072]{1,0:T(8,128)}), f32[8,3072]{1,0:T(8,128)}) %all-reduce.7.cloned.1.call-update) | async-done | bytes 98320 | tf_op jit(solution)/shard_map/psum | solution.py:58
  89.1 128.7 %scatter_custom_fusion = f32[262144]{0:T(1024)S(1)} fusion(s32[24576]{0:T(1024)S(1)} %bitcast.33, f32[24576]{0:T(1024)S(1)} %bitcast.34, f32[]{:T(128)} %constant.72.clone.1), kind=kCustom, calls=%fused_computation.56 | custom fusion | flops 24576 | bytes 1048580 | tf_op jit(solution)/shard_map/scatter-add | solution.py:63
  217.8 1.3 reshape.32
  219.1 2.1 multiply_add_fusion.2
  221.2 1.3 collective-permute-start.1
  222.5 1.4 collective-permute-start
  223.9 3.5 collective-permute-done
  227.5 1.3 collective-permute-start.2
  228.8 4.5 collective-permute-start.3
  233.9 1.5 collective-permute-done.3
  235.4 1.2 select_maximum_fusion.4
  236.7 2.6 multiply_reduce_fusion.1
  239.3 42.2 %all-reduce.3 = (f32[]{:T(128)}, f32[]{:T(128)}) all-reduce(f32[]{:T(128)} %get-tuple-element.7, f32[]{:T(128)} %get-tuple-element.6), channel_id=1, replica_groups=mesh['energy'=8,'kpt'=4] {'energy','kpt'}, use_global_device_ids=true, to_apply=%region_4.5 | all-reduce | flops 2 | bytes 16 | tf_op jit(solution)/shard_map/psum | solution.py:35
  282.8 1.5 multiply_subtract_fusion
  284.3 1.3 collective-permute-start.5
  285.6 1.3 collective-permute-start.4
  286.9 4.2 collective-permute-done.4
  291.3 1.4 collective-permute-start.6
  292.8 4.5 collective-permute-start.7
  297.8 1.5 collective-permute-done.7
  299.3 1.3 select_maximum_fusion
  300.6 1.7 fusion.7
  302.3 42.7 %all-reduce.2 = (f32[]{:T(128)}, f32[]{:T(128)}) all-reduce(f32[]{:T(128)} %get-tuple-element.5, f32[]{:T(128)} %get-tuple-element.4), channel_id=1, replica_groups=mesh['energy'=8,'kpt'=4] {'energy','kpt'}, use_global_device_ids=true, to_apply=%region_8.9 | all-reduce | flops 2 | bytes 16 | tf_op jit(solution)/shard_map/psum | solution.py:35
  349.4 1.5 multiply_add_fusion
  352.4 135.5 %gather_fusion = f32[24576]{0:T(1024)S(1)} fusion(f32[262144]{0:T(1024)S(1)} %bitcast.27, s32[24576]{0:T(1024)S(1)} %broadcast_clamp_fusion), kind=kCustom, calls=%fused_computation | custom fusion | bytes 294912 | tf_op jit(solution)/shard_map/jit(_take)/gather | solution.py:90
  488.7 35.5 %all-reduce.9.cloned.1.call-done = f32[8,3072]{1,0:T(8,128)} async-done(((f32[8,3072]{1,0:T(8,128)}), f32[8,3072]{1,0:T(8,128)}) %all-reduce.9.cloned.1.call-update) | async-done | bytes 98320 | tf_op jit(solution)/shard_map/psum | solution.py:91
  524.2 10.7 %all_gather.3 = f32[64,3072]{1,0:T(8,128)S(1)} all-gather(f32[8,3072]{1,0:T(8,128)} %all-reduce.9.cloned.1.call-done), channel_id=1, replica_groups=mesh['energy'=8,'kpt'=4] {'energy'}, dimensions={0}, use_global_device_ids=true | all-gather | bytes 884736 | tf_op jit(solution)/shard_map/all_gather | solution.py:98
  534.8 7.3 %fusion.1 = f32[64,1,4]{2,1,0:T(1,128)S(1)} fusion(bf16[4,64,3072]{2,1,0:T(8,128)(2,1)S(1)} %bitcast.26, f32[64,3072,1]{1,0,2:T(8,128)S(1)} %bitcast.31), kind=kOutput, calls=%fused_computation.13 | convolution fusion | flops 9437184 | bytes 2360320 | tf_op jit(solution)/shard_map/eklo,lo->ekl/dot_general | solution.py:95
  (46 shorter events, 6.5 us)
Async XLA Ops:
  7.2 1.4 copy-start
  7.2 44.0 %reduce-scatter.2.cloned.1.call-start = ((), (), s32[]{:S(2)}) async-start(), calls=%async_computation.1 | async-start | bytes 884736 | tf_op jit(solution)/shard_map/reduce_scatter | solution.py:57
  8.6 42.7 %copy-start.5 = (f32[64]{0:T(128)S(1)}, f32[64]{0:T(128)}, u32[]{:S(2)}) copy-start(f32[64]{0:T(128)} %param.11) | copy-start | bytes 772
  13.4 74.6 %all-reduce.7.cloned.1.call-start = ((), (), s32[]{:S(2)}) async-start(), calls=%async_computation.2 | async-start | bytes 196608 | tf_op jit(solution)/shard_map/psum | solution.py:58
  51.2 472.9 %all-reduce.9.cloned.1.call-start = ((), (), s32[]{:S(2)}) async-start(), calls=%async_computation.3 | async-start | bytes 196608 | tf_op jit(solution)/shard_map/psum | solution.py:91
  221.2 2.7 collective-permute-start.1
  222.5 14.2 %copy-start.2 = (s32[64,16,256]{2,1,0:T(8,128)S(1)}, s32[64,16,256]{2,1,0:T(8,128)}, u32[]{:S(2)}) copy-start(s32[64,16,256]{2,1,0:T(8,128)} %param.10) | copy-start | bytes 3145732
  222.5 4.9 collective-permute-start
  227.5 6.2 %collective-permute-start.2 = (f32[66,1,256]{2,0,1:T(8,128)S(1)}, f32[66,1,256]{2,0,1:T(8,128)S(1)}, u32[]{:S(2)}, u32[]{:S(2)}) collective-permute-start(f32[66,1,256]{2,0,1:T(8,128)S(1)} %copy.11), channel_id=1, source_target_pairs={{1,0},{2,1},{3,2},{5,4},{6,5},{7,6},{9,8},{10,9},{11,10},{13,12},{... | collective-permute-start | bytes 202760 | tf_op jit(solution)/shard_map/ppermute | solution.py:20
  228.8 6.5 %collective-permute-start.3 = (f32[66,1,256]{2,0,1:T(8,128)S(1)}, f32[66,1,256]{2,0,1:T(8,128)S(1)}, u32[]{:S(2)}, u32[]{:S(2)}) collective-permute-start(f32[66,1,256]{2,0,1:T(8,128)S(1)} %copy.13), channel_id=1, source_target_pairs={{0,1},{1,2},{2,3},{4,5},{5,6},{6,7},{8,9},{9,10},{10,11},{12,13},{... | collective-permute-start | bytes 202760 | tf_op jit(solution)/shard_map/ppermute | solution.py:17
  284.3 16.3 %copy-start.1 = (f32[64,16,256]{2,1,0:T(8,128)}, f32[64,16,256]{2,1,0:T(8,128)S(1)}, u32[]{:S(2)}) copy-start(f32[64,16,256]{2,1,0:T(8,128)S(1)} %multiply_subtract_fusion) | copy-start | bytes 3145732
  284.3 2.6 collective-permute-start.5
  285.6 5.6 %collective-permute-start.4 = (f32[1,16,256]{2,1,0:T(8,128)S(1)}, f32[1,16,256]{2,1,0:T(8,128)S(1)}, u32[]{:S(2)}, u32[]{:S(2)}) collective-permute-start(f32[1,16,256]{2,1,0:T(8,128)S(1)} %get-tuple-element.23), channel_id=1, source_target_pairs={{4,0},{8,4},{12,8},{16,12},{20,16},{24,20},{28,24},{5,1},{9,5},{13... | collective-permute-start | bytes 49160 | tf_op jit(solution)/shard_map/ppermute | solution.py:20
  291.3 9.3 %copy-start.3 = (s32[64,16,256]{2,1,0:T(8,128)S(1)}, s32[64,16,256]{2,1,0:T(8,128)}, u32[]{:S(2)}) copy-start(s32[64,16,256]{2,1,0:T(8,128)} %param.10) | copy-start | bytes 3145732
  291.3 6.4 %collective-permute-start.6 = (f32[66,1,256]{2,0,1:T(8,128)S(1)}, f32[66,1,256]{2,0,1:T(8,128)S(1)}, u32[]{:S(2)}, u32[]{:S(2)}) collective-permute-start(f32[66,1,256]{2,0,1:T(8,128)S(1)} %copy.17), channel_id=1, source_target_pairs={{1,0},{2,1},{3,2},{5,4},{6,5},{7,6},{9,8},{10,9},{11,10},{13,12},{... | collective-permute-start | bytes 202760 | tf_op jit(solution)/shard_map/ppermute | solution.py:20
  292.8 6.5 %collective-permute-start.7 = (f32[66,1,256]{2,0,1:T(8,128)S(1)}, f32[66,1,256]{2,0,1:T(8,128)S(1)}, u32[]{:S(2)}, u32[]{:S(2)}) collective-permute-start(f32[66,1,256]{2,0,1:T(8,128)S(1)} %copy.19), channel_id=1, source_target_pairs={{0,1},{1,2},{2,3},{4,5},{5,6},{6,7},{8,9},{9,10},{10,11},{12,13},{... | collective-permute-start | bytes 202760 | tf_op jit(solution)/shard_map/ppermute | solution.py:17
  350.9 1.0 copy-start.4
Sparse Core Ops, SparseCore 0:
  13.5 37.6 reduce-scatter.1
  53.5 34.4 all-reduce.6
  488.8 35.3 all-reduce.8
where the time goes:
time: 550 us; the launch traced here: 549 us
  other arithmetic  144 us (26%)
  local copies, waits for them, and re-layouts  141 us (26%)
  waiting for transfers between devices  120 us (22%)
  blocking collectives  95.6 us (17%)
  between operations  19.7 us (4%)
  starting transfers between devices  17.2 us (3%)
  matrix products  11.1 us (2%)
    gather x2, local copies, waits for them, and re-layouts, per_device(): jnp.take(potential.reshape(-1), flat_cell)  136 us
    scatter-add x1, other arithmetic, per_device(): jax.ops.segment_sum(jnp.where(inside, slab_occupancy, 0.0).reshape(-1), f...  129 us
    psum x2, blocking collectives, paired_sums(): lax.psum((jnp.sum(residual * residual), jnp.sum(residual * image)), ('ene...  84.9 us
    psum x1, waiting for transfers between devices, per_device(): slab_occupancy = lax.psum(partial_rows, 'kpt')  36.7 us
    reduce_scatter x1, waiting for transfers between devices, per_device(): lax.psum_scatter(occupancy, 'energy', scatter_dimension=0, tiled=True)  36.6 us
    psum x1, waiting for transfers between devices, per_device(): orbital_potential = lax.psum(local_values, 'kpt')  35.5 us
    ppermute x4, starting transfers between devices, with_halo(): lax.ppermute(lax.slice_in_dim(block, block.shape[dim] - width, None, axis...  11.7 us
  transfers between devices with their start and end apart: 11, of which 9 were waited for; matrix products, arithmetic and copies ran while one was open for 0% of the time, Pallas kernels for 0%

commit v1 on v0

--- a/solution.py
+++ b/solution.py
@@ -88,7 +88,14 @@
             along = image + ratio * along
             norm_now = norm_next
     local_values = jnp.where(inside, jnp.take(potential.reshape(-1), flat_cell), 0.0)
-    orbital_potential = lax.psum(local_values, "kpt")
+    num_devices = lax.axis_size("kpt")
+    orbital_potential = local_values
+    for it in [
+        [(d, d ^ dev) for d in range(num_devices)] for dev in (1, 2, 4, 8, 16) if dev < num_devices
+    ]:
+        orbital_potential = orbital_potential + lax.ppermute(
+            orbital_potential, axis_name="kpt", perm=it
+        )
     factor = density.shape[3] ** (-0.5)
     block = density.astype(jnp.float32)
     band_shift = (

time: 550 us -> 527 us (0.958)
  waiting for transfers between devices: 120 us -> 92.6 us
    psum x1 -> x0, waiting for transfers between devices: 35.5 us -> none  [per_device(): orbital_potential = lax.psum(local_values, 'kpt')]
    ppermute x0 -> x2, waiting for transfers between devices: none -> 7.8 us  [per_device(): lax.ppermute(orbital_potential, axis_name='kpt', perm=it)]
  transfers between devices with their start and end apart: 11 -> 12, of which waited for: 9 -> 10; matrix products, arithmetic and copies ran while one was open for 0% -> 0% of each run, Pallas kernels for 0% -> 0%
where the time goes in v1:
time: 527 us; the launch traced here: 526 us
  other arithmetic  144 us (27%)
  local copies, waits for them, and re-layouts  141 us (27%)
  blocking collectives  96.3 us (18%)
  waiting for transfers between devices  92.6 us (18%)
  starting transfers between devices  20.7 us (4%)
  between operations  20.1 us (4%)
  matrix products  11.1 us (2%)
    gather x2, local copies, waits for them, and re-layouts, per_device(): jnp.take(potential.reshape(-1), flat_cell)  136 us
    scatter-add x1, other arithmetic, per_device(): jax.ops.segment_sum(jnp.where(inside, slab_occupancy, 0.0).reshape(-1), f...  129 us
    psum x2, blocking collectives, paired_sums(): lax.psum((jnp.sum(residual * residual), jnp.sum(residual * image)), ('ene...  84.9 us
    psum x1, waiting for transfers between devices, per_device(): slab_occupancy = lax.psum(partial_rows, 'kpt')  36.7 us
    reduce_scatter x1, waiting for transfers between devices, per_device(): lax.psum_scatter(occupancy, 'energy', scatter_dimension=0, tiled=True)  36.6 us
    ppermute x4, starting transfers between devices, with_halo(): lax.ppermute(lax.slice_in_dim(block, block.shape[dim] - width, None, axis...  11.7 us
    all_gather x1, blocking collectives, per_device(): lax.all_gather(orbital_potential, 'energy', axis=0, tiled=True)  11.4 us
  transfers between devices with their start and end apart: 12, of which 10 were waited for; matrix products, arithmetic and copies ran while one was open for 0% of the time, Pallas kernels for 0%

profile of v1, /device:TPU:0, one launch (start us, length us, event | category | flops | bytes accessed | tf_op | source)
XLA Modules:
  0.0 525.7 jit_solution(5177708503255093533)
XLA Ops:
  7.2 1.4 copy-done
  8.6 3.8 fusion.3
  14.6 36.6 %reduce-scatter.2.cloned.1.call-done = f32[8,3072]{1,0:T(8,128)} async-done(((f32[64,3072]{1,0:T(8,128)}), f32[8,3072]{1,0:T(8,128)}) %reduce-scatter.2.cloned.1.call-update) | async-done | bytes 98320 | tf_op jit(solution)/shard_map/reduce_scatter | solution.py:57
  51.3 36.7 %all-reduce.6.cloned.1.call-done = f32[8,3072]{1,0:T(8,128)} async-done(((f32[8,3072]{1,0:T(8,128)}), f32[8,3072]{1,0:T(8,128)}) %all-reduce.6.cloned.1.call-update) | async-done | bytes 98320 | tf_op jit(solution)/shard_map/psum | solution.py:58
  89.1 128.7 %scatter_custom_fusion = f32[262144]{0:T(1024)S(1)} fusion(s32[24576]{0:T(1024)S(1)} %bitcast.33, f32[24576]{0:T(1024)S(1)} %bitcast.34, f32[]{:T(128)} %constant.72.clone.1), kind=kCustom, calls=%fused_computation.56 | custom fusion | flops 24576 | bytes 1048580 | tf_op jit(solution)/shard_map/scatter-add | solution.py:63
  217.8 1.3 reshape.32
  219.1 2.1 multiply_add_fusion.2
  221.2 1.3 collective-permute-start.1
  222.5 1.4 collective-permute-start
  223.9 3.5 collective-permute-done
  227.5 1.3 collective-permute-start.2
  228.8 4.5 collective-permute-start.3
  233.9 1.5 collective-permute-done.3
  236.7 2.7 multiply_reduce_fusion.1
  239.4 42.2 %all-reduce.3 = (f32[]{:T(128)}, f32[]{:T(128)}) all-reduce(f32[]{:T(128)} %get-tuple-element.7, f32[]{:T(128)} %get-tuple-element.6), channel_id=1, replica_groups=mesh['energy'=8,'kpt'=4] {'energy','kpt'}, use_global_device_ids=true, to_apply=%region_4.5 | all-reduce | flops 2 | bytes 16 | tf_op jit(solution)/shard_map/psum | solution.py:35
  282.8 1.5 multiply_subtract_fusion
  284.3 1.3 collective-permute-start.5
  285.6 1.3 collective-permute-start.4
  287.0 4.2 collective-permute-done.4
  291.4 1.4 collective-permute-start.6
  292.8 4.5 collective-permute-start.7
  297.8 1.5 collective-permute-done.7
  300.7 1.7 fusion.7
  302.3 42.7 %all-reduce.2 = (f32[]{:T(128)}, f32[]{:T(128)}) all-reduce(f32[]{:T(128)} %get-tuple-element.5, f32[]{:T(128)} %get-tuple-element.4), channel_id=1, replica_groups=mesh['energy'=8,'kpt'=4] {'energy','kpt'}, use_global_device_ids=true, to_apply=%region_8.9 | all-reduce | flops 2 | bytes 16 | tf_op jit(solution)/shard_map/psum | solution.py:35
  349.5 1.5 multiply_add_fusion
  352.5 135.5 %gather_fusion = f32[24576]{0:T(1024)S(1)} fusion(f32[262144]{0:T(1024)S(1)} %bitcast.27, s32[24576]{0:T(1024)S(1)} %broadcast_clamp_fusion), kind=kCustom, calls=%fused_computation | custom fusion | bytes 294912 | tf_op jit(solution)/shard_map/jit(_take)/gather | solution.py:90
  488.1 1.4 collective-permute-start.8
  489.5 3.3 collective-permute-done.8
  492.8 2.1 collective-permute-start.9
  494.9 4.5 collective-permute-done.9
  499.4 11.4 %all_gather.3 = f32[64,3072]{1,0:T(8,128)S(1)} all-gather(f32[8,3072]{1,0:T(8,128)S(1)} %add.125), channel_id=1, replica_groups=mesh['energy'=8,'kpt'=4] {'energy'}, dimensions={0}, use_global_device_ids=true | all-gather | bytes 884736 | tf_op jit(solution)/shard_map/all_gather | solution.py:105
  510.9 7.3 %fusion.1 = f32[64,1,4]{2,1,0:T(1,128)S(1)} fusion(bf16[4,64,3072]{2,1,0:T(8,128)(2,1)S(1)} %bitcast.26, f32[64,3072,1]{1,0,2:T(8,128)S(1)} %bitcast.31), kind=kOutput, calls=%fused_computation.13 | convolution fusion | flops 9437184 | bytes 2360320 | tf_op jit(solution)/shard_map/eklo,lo->ekl/dot_general | solution.py:102
  (49 shorter events, 9.5 us)
Async XLA Ops:
  7.2 1.4 copy-start
  7.2 44.0 %reduce-scatter.2.cloned.1.call-start = ((), (), s32[]{:S(2)}) async-start(), calls=%async_computation.1 | async-start | bytes 884736 | tf_op jit(solution)/shard_map/reduce_scatter | solution.py:57
  8.6 42.7 %copy-start.5 = (f32[64]{0:T(128)S(1)}, f32[64]{0:T(128)}, u32[]{:S(2)}) copy-start(f32[64]{0:T(128)} %param.11) | copy-start | bytes 772
  13.4 74.6 %all-reduce.6.cloned.1.call-start = ((), (), s32[]{:S(2)}) async-start(), calls=%async_computation.2 | async-start | bytes 196608 | tf_op jit(solution)/shard_map/psum | solution.py:58
  221.2 2.7 collective-permute-start.1
  222.5 14.2 %copy-start.2 = (s32[64,16,256]{2,1,0:T(8,128)S(1)}, s32[64,16,256]{2,1,0:T(8,128)}, u32[]{:S(2)}) copy-start(s32[64,16,256]{2,1,0:T(8,128)} %param.10) | copy-start | bytes 3145732
  222.5 4.9 collective-permute-start
  227.5 6.2 %collective-permute-start.2 = (f32[66,1,256]{2,0,1:T(8,128)S(1)}, f32[66,1,256]{2,0,1:T(8,128)S(1)}, u32[]{:S(2)}, u32[]{:S(2)}) collective-permute-start(f32[66,1,256]{2,0,1:T(8,128)S(1)} %copy.11), channel_id=1, source_target_pairs={{1,0},{2,1},{3,2},{5,4},{6,5},{7,6},{9,8},{10,9},{11,10},{13,12},{... | collective-permute-start | bytes 202760 | tf_op jit(solution)/shard_map/ppermute | solution.py:20
  228.8 6.5 %collective-permute-start.3 = (f32[66,1,256]{2,0,1:T(8,128)S(1)}, f32[66,1,256]{2,0,1:T(8,128)S(1)}, u32[]{:S(2)}, u32[]{:S(2)}) collective-permute-start(f32[66,1,256]{2,0,1:T(8,128)S(1)} %copy.13), channel_id=1, source_target_pairs={{0,1},{1,2},{2,3},{4,5},{5,6},{6,7},{8,9},{9,10},{10,11},{12,13},{... | collective-permute-start | bytes 202760 | tf_op jit(solution)/shard_map/ppermute | solution.py:17
  284.3 16.3 %copy-start.1 = (f32[64,16,256]{2,1,0:T(8,128)}, f32[64,16,256]{2,1,0:T(8,128)S(1)}, u32[]{:S(2)}) copy-start(f32[64,16,256]{2,1,0:T(8,128)S(1)} %multiply_subtract_fusion) | copy-start | bytes 3145732
  284.3 2.6 collective-permute-start.5
  285.6 5.6 %collective-permute-start.4 = (f32[1,16,256]{2,1,0:T(8,128)S(1)}, f32[1,16,256]{2,1,0:T(8,128)S(1)}, u32[]{:S(2)}, u32[]{:S(2)}) collective-permute-start(f32[1,16,256]{2,1,0:T(8,128)S(1)} %get-tuple-element.23), channel_id=1, source_target_pairs={{4,0},{8,4},{12,8},{16,12},{20,16},{24,20},{28,24},{5,1},{9,5},{13... | collective-permute-start | bytes 49160 | tf_op jit(solution)/shard_map/ppermute | solution.py:20
  291.3 9.3 %copy-start.3 = (s32[64,16,256]{2,1,0:T(8,128)S(1)}, s32[64,16,256]{2,1,0:T(8,128)}, u32[]{:S(2)}) copy-start(s32[64,16,256]{2,1,0:T(8,128)} %param.10) | copy-start | bytes 3145732
  291.4 6.4 %collective-permute-start.6 = (f32[66,1,256]{2,0,1:T(8,128)S(1)}, f32[66,1,256]{2,0,1:T(8,128)S(1)}, u32[]{:S(2)}, u32[]{:S(2)}) collective-permute-start(f32[66,1,256]{2,0,1:T(8,128)S(1)} %copy.17), channel_id=1, source_target_pairs={{1,0},{2,1},{3,2},{5,4},{6,5},{7,6},{9,8},{10,9},{11,10},{13,12},{... | collective-permute-start | bytes 202760 | tf_op jit(solution)/shard_map/ppermute | solution.py:20
  292.8 6.5 %collective-permute-start.7 = (f32[66,1,256]{2,0,1:T(8,128)S(1)}, f32[66,1,256]{2,0,1:T(8,128)S(1)}, u32[]{:S(2)}, u32[]{:S(2)}) collective-permute-start(f32[66,1,256]{2,0,1:T(8,128)S(1)} %copy.19), channel_id=1, source_target_pairs={{0,1},{1,2},{2,3},{4,5},{5,6},{6,7},{8,9},{9,10},{10,11},{12,13},{... | collective-permute-start | bytes 202760 | tf_op jit(solution)/shard_map/ppermute | solution.py:17
  350.9 1.0 copy-start.4
  488.1 4.7 collective-permute-start.8
  492.8 6.6 %collective-permute-start.9 = (f32[8,3072]{1,0:T(8,128)S(1)}, f32[8,3072]{1,0:T(8,128)S(1)}, u32[]{:S(2)}, u32[]{:S(2)}) collective-permute-start(f32[8,3072]{1,0:T(8,128)S(1)} %add.124), channel_id=1, source_target_pairs={{0,2},{1,3},{2,0},{3,1},{4,6},{5,7},{6,4},{7,5},{8,10},{9,11},{10,... | collective-permute-start | bytes 294920 | tf_op jit(solution)/shard_map/ppermute | solution.py:96
Sparse Core Ops, SparseCore 0:
  13.5 37.6 reduce-scatter.1
  53.5 34.4 all-reduce.5
